TPU v7x, 256 devices: a whole 4x4x8 slice. The times are simulated.
256 devices in a mesh: row: 16 (over z, y_hi), col: 16 (over y_lo, x, core).
Axes of the slice: x: 4, y: 4 (y_hi: 2, y_lo: 2; y = y_hi * 2 + y_lo), z: 8, core: 2. Of those that a mesh axis runs over, the one named last changes fastest.
Arguments:
- object_field: float32 [2, 4096, 4096], P(None, 'row', 'col'), may hold values from -5 to 5
- probe: float32 [2, 256, 256], replicated, may hold values from -6 to 6
- amplitudes: float32 [16, 16, 4, 256, 256], P('row', 'col'), may hold values from 0 to 11, as said below
- positions: int32 [16, 16, 4, 2], P('row', 'col'), may hold values from 0 to 64
Outputs:
- object_next: float32 [2, 4096, 4096], P(None, 'row', 'col')
- probe_next: float32 [2, 256, 256], replicated
Inputs may be any that keep to these rules, and one draw needn't show every extreme that they name: Positive amplitudes.
All inputs are finite; a program needn't handle non-finite values.
Results may differ from a plain program's by a relative error of at most 0.0003.
Values sent between devices are 32-bit elements; how exact they have to be, the bound alone decides.
A program may use at most 64 MiB of HBM per device.

v0:
```python
import math
import jax
import jax.numpy as jnp
from jax import lax
from jax.sharding import PartitionSpec as P

W = 256
MARGIN = 32
smoothing = 0.1
regular = 1.0
epsilon = 1e-06


def padded(block, sides, width):
    for axis, dim in sides:
        count = lax.axis_size(axis)
        forward = [(i, i + 1) for i in range(count - 1)]
        backward = [(target, source) for source, target in forward]
        low = lax.ppermute(
            lax.slice_in_dim(block, block.shape[dim] - width, None, axis=dim), axis, forward
        )
        high = lax.ppermute(lax.slice_in_dim(block, 0, width, axis=dim), axis, backward)
        block = jnp.concatenate([low, block, high], axis=dim)
    return block


def shifted(block, axis, distance):
    devices = range(lax.axis_size(axis))
    route = [(i - distance, i) for i in devices if i - distance in devices]
    return lax.ppermute(block, axis, route)


def tables(length):
    indices = jnp.arange(length, dtype=jnp.int32)
    phases = (indices[:, None] * indices[None, :] % length).astype(jnp.float32) * (
        2.0 * math.pi / length
    )
    scaling = 1.0 / math.sqrt(length)
    cosine = jnp.cos(phases) * scaling
    sines = jnp.sin(phases) * scaling
    forward = jnp.concatenate(
        [jnp.concatenate([cosine, sines], 1), jnp.concatenate([-sines, cosine], 1)], 0
    )
    inverse = jnp.concatenate(
        [jnp.concatenate([cosine, -sines], 1), jnp.concatenate([sines, cosine], 1)], 0
    )
    return (forward, inverse)


def transform(wavefield, left_matrix, right_matrix):
    length = wavefield.shape[1]
    stacked = wavefield.reshape(2 * length, length)
    mixed = jnp.dot(left_matrix, stacked, precision=lax.Precision.HIGHEST)
    paired = jnp.concatenate([mixed[:length], mixed[length:]], axis=1)
    result = jnp.dot(paired, right_matrix, precision=lax.Precision.HIGHEST)
    return jnp.stack([result[:, :length], result[:, length:]])


def frame_terms(probe, window, amplitude, forward, inverse):
    exit_real = probe[0] * window[0] - probe[1] * window[1]
    exit_imag = probe[0] * window[1] + probe[1] * window[0]
    wave = jnp.stack([exit_real, exit_imag])
    far_field = transform(wave, forward, inverse)
    factor = amplitude / jnp.sqrt(
        far_field[0] * far_field[0] + far_field[1] * far_field[1] + smoothing
    )
    near_field = transform(far_field * factor[None], inverse, forward)
    difference = near_field - wave
    object_real = probe[0] * difference[0] + probe[1] * difference[1]
    object_imag = probe[0] * difference[1] - probe[1] * difference[0]
    probe_real = window[0] * difference[0] + window[1] * difference[1]
    probe_imag = window[0] * difference[1] - window[1] * difference[0]
    window_power = window[0] * window[0] + window[1] * window[1]
    return (
        jnp.stack([object_real, object_imag]),
        jnp.stack([probe_real, probe_imag, window_power]),
    )


def add_edges(middle, leading, trailing, along, tile_side, margin):
    head_pad = [(0, 0), (0, 0), (0, 0)]
    tail_pad = [(0, 0), (0, 0), (0, 0)]
    head_pad[along] = (0, tile_side - margin)
    tail_pad[along] = (tile_side - margin, 0)
    return middle + jnp.pad(leading, head_pad) + jnp.pad(trailing, tail_pad)


def per_device(object_field, probe, amplitudes, positions):
    forward, inverse = tables(W)
    tile_side = object_field.shape[1]
    margin = MARGIN
    window_side = tile_side + 2 * margin
    extended = padded(object_field, (("row", 1), ("col", 2)), MARGIN)
    power_map = probe[0] * probe[0] + probe[1] * probe[1]
    measured = amplitudes[0, 0]
    offsets = positions[0, 0]
    frame_total = measured.shape[0]
    anchor = jnp.zeros((), jnp.int32)

    def visit(frame_index, carried):
        canvas, probe_acc = carried
        amplitude = measured[frame_index]
        offset = offsets[frame_index]
        window = lax.dynamic_slice(extended, (anchor, offset[0], offset[1]), (2, W, W))
        object_term, probe_term = frame_terms(probe, window, amplitude, forward, inverse)
        update = jnp.concatenate([object_term, power_map[None]], 0)
        current = lax.dynamic_slice(canvas, (anchor, offset[0], offset[1]), (3, W, W))
        canvas = lax.dynamic_update_slice(canvas, current + update, (anchor, offset[0], offset[1]))
        return (canvas, probe_acc + probe_term)

    canvas_start = jnp.zeros((3, window_side, window_side), jnp.float32)
    probe_start = jnp.zeros((3, W, W), jnp.float32)
    canvas, probe_acc = lax.fori_loop(0, frame_total, visit, (canvas_start, probe_start))
    from_above = shifted(canvas[:, window_side - margin :, :], "row", 1)
    from_below = shifted(canvas[:, :margin, :], "row", -1)
    row_folded = add_edges(
        canvas[:, margin : margin + tile_side, :], from_above, from_below, 1, tile_side, margin
    )
    from_before = shifted(row_folded[:, :, window_side - margin :], "col", 1)
    from_after = shifted(row_folded[:, :, :margin], "col", -1)
    folded = add_edges(
        row_folded[:, :, margin : margin + tile_side], from_before, from_after, 2, tile_side, margin
    )
    object_next = object_field + folded[0:2] / (folded[2] + regular)
    local_target = jnp.sum(measured * measured)
    devices = lax.axis_size("row") * lax.axis_size("col")
    frame_count = frame_total * devices
    totals, target_sum = lax.psum((probe_acc, local_target), ("row", "col"))
    stepped = probe + totals[0:2] / (totals[2] + regular)
    probe_power = jnp.sum(stepped * stepped)
    target = target_sum / frame_count
    probe_next = stepped * jnp.sqrt(target / (probe_power + epsilon))
    return (object_next, probe_next)


def solution(mesh):
    return jax.shard_map(
        per_device,
        mesh=mesh,
        in_specs=(
            P(None, "row", "col"),
            P(),
            P("row", "col", None, None, None),
            P("row", "col", None, None),
        ),
        out_specs=(P(None, "row", "col"), P()),
        check_vma=False,
    )
```

profile of v0, /device:TPU:2, one launch (start us, length us, event | category | flops | bytes accessed | tf_op | source)
XLA Modules:
  0.0 516.5 jit_solution(1246306254406606753)
XLA Ops:
  8.2 5.1 collective-permute-start
  15.6 1.8 add_bitcast_fusion
  18.5 2.5 collective-permute-done.1
  21.9 1.9 collective-permute-start.2
  23.8 3.6 collective-permute-start.3
  27.7 2.9 collective-permute-done.2
  30.6 1.8 collective-permute-done.3
  32.3 2.4 pad_maximum_fusion.5
  36.0 107.6 %while.16 = (s32[]{:T(128)}, f32[3,320,320]{2,1,0:T(8,128)}, f32[3,256,256]{2,1,0:T(8,128)}, s32[4,2]{0,1:T(2,128)S(1)}, f32[2,256,256]{2,1,0:T(8,128)S(1)}, /*i...) while((s32[]{:T(128)}, f32[3,320,320]{2,1,0:T(8,128)}, ...), condition=%wide.region_1.2_spmd.clone, body=%wide.region_0.1_spmd.clone.sunk | while | flops 3225354240 | bytes 31064388 | solution.py:113
  41.9 1.9 convolution_bitcast_fusion.4
  45.9 1.9 convolution_bitcast_fusion.5
  51.4 2.9 maximum_add_fusion.3
  54.3 8.7 %dynamic_update_slice.9 = f32[3,320,320]{2,1,0:T(8,128)} dynamic-update-slice(f32[3,320,320]{2,1,0:T(8,128)} %get-tuple-element.377, f32[3,256,256]{2,1,0:T(8,128)S(1)} %get-tuple-element.360, s32[]{:T(128)} %constant.57.clone.1..sunk, s32[]{:T(128)S(6)} %select_n.61, s32[]{:T(128)S(6)} %select_n.62) | dynamic-update-slice | bytes 1572868 | tf_op jit(solution)/shard_map/while/body/eval_jaxpr/dynamic_update_slice | solution.py:108
  68.9 1.9 convolution_bitcast_fusion.4
  73.0 1.9 convolution_bitcast_fusion.5
  78.5 3.2 maximum_add_fusion.3
  81.7 8.5 %dynamic_update_slice.9 = f32[3,320,320]{2,1,0:T(8,128)} dynamic-update-slice(f32[3,320,320]{2,1,0:T(8,128)} %get-tuple-element.377, f32[3,256,256]{2,1,0:T(8,128)S(1)} %get-tuple-element.360, s32[]{:T(128)} %constant.57.clone.1..sunk, s32[]{:T(128)S(6)} %select_n.61, s32[]{:T(128)S(6)} %select_n.62) | dynamic-update-slice | bytes 1572868 | tf_op jit(solution)/shard_map/while/body/eval_jaxpr/dynamic_update_slice | solution.py:108
  96.1 1.9 convolution_bitcast_fusion.4
  100.1 1.9 convolution_bitcast_fusion.5
  105.6 3.2 maximum_add_fusion.3
  108.8 8.5 %dynamic_update_slice.9 = f32[3,320,320]{2,1,0:T(8,128)} dynamic-update-slice(f32[3,320,320]{2,1,0:T(8,128)} %get-tuple-element.377, f32[3,256,256]{2,1,0:T(8,128)S(1)} %get-tuple-element.360, s32[]{:T(128)} %constant.57.clone.1..sunk, s32[]{:T(128)S(6)} %select_n.61, s32[]{:T(128)S(6)} %select_n.62) | dynamic-update-slice | bytes 1572868 | tf_op jit(solution)/shard_map/while/body/eval_jaxpr/dynamic_update_slice | solution.py:108
  123.2 1.9 convolution_bitcast_fusion.4
  127.3 1.9 convolution_bitcast_fusion.5
  132.7 3.2 maximum_add_fusion.3
  135.9 7.6 %dynamic_update_slice.9 = f32[3,320,320]{2,1,0:T(8,128)} dynamic-update-slice(f32[3,320,320]{2,1,0:T(8,128)} %get-tuple-element.377, f32[3,256,256]{2,1,0:T(8,128)S(1)} %get-tuple-element.360, s32[]{:T(128)} %constant.57.clone.1..sunk, s32[]{:T(128)S(6)} %select_n.61, s32[]{:T(128)S(6)} %select_n.62) | dynamic-update-slice | bytes 1572868 | tf_op jit(solution)/shard_map/while/body/eval_jaxpr/dynamic_update_slice | solution.py:108
  144.5 5.3 %collective-permute-start.4 = (f32[3,32,320]{2,1,0:T(8,128)S(1)}, f32[3,32,320]{2,1,0:T(8,128)S(1)}, u32[]{:S(2)}, u32[]{:S(2)}) collective-permute-start(f32[3,32,320]{2,1,0:T(8,128)S(1)} %get-tuple-element.249), channel_id=1, source_target_pairs={{0,16},{16,32},{32,48},{48,64},{64,80},{80,96},{96,112},{112,128},... | collective-permute-start | bytes 368648 | tf_op jit(solution)/shard_map/ppermute | solution.py:30
  152.9 6.3 %collective-permute-done.5 = f32[3,32,320]{2,1,0:T(8,128)S(1)} collective-permute-done((f32[3,32,320]{2,1,0:T(8,128)S(1)}, f32[3,32,320]{2,1,0:T(8,128)S(1)}, u32[]{:S(2)}, u32[]{:S(2)}) %collective-permute-start.5) | collective-permute-done | bytes 122912 | tf_op jit(solution)/shard_map/ppermute | solution.py:30
  160.8 2.6 collective-permute-start.6
  163.4 3.0 collective-permute-start.7
  167.3 81.6 %psum.15 = f32[]{:T(128)} all-reduce(f32[]{:T(128)} %multiply_reduce_fusion), channel_id=1, replica_groups=mesh['row'=16,'col'=16] {'row','col'}, use_global_device_ids=true, to_apply=%region_4.5 | all-reduce | flops 1 | bytes 8 | tf_op jit(solution)/shard_map/psum | solution.py:128
  251.4 253.7 %all-reduce.6.cloned.1.call-done = f32[3,256,256]{2,1,0:T(8,128)} async-done(((f32[3,256,256]{2,1,0:T(8,128)}), f32[3,256,256]{2,1,0:T(8,128)}) %all-reduce.6.cloned.1.call-update) | async-done | bytes 786448 | tf_op jit(solution)/shard_map/psum | solution.py:128
  506.2 1.8 multiply_reduce_fusion.1
  (99 shorter events, 47.8 us)
Async XLA Ops:
  7.2 11.3 %copy-start.3 = (f32[2,256,256]{2,1,0:T(8,128)S(1)}, f32[2,256,256]{2,1,0:T(8,128)}, u32[]{:S(2)}) copy-start(f32[2,256,256]{2,1,0:T(8,128)} %param.6) | copy-start | bytes 1572868
  7.2 498.0 %all-reduce.6.cloned.1.call-start = ((), (), s32[]{:S(2)}) async-start(), calls=%async_computation | async-start | bytes 1572864 | tf_op jit(solution)/shard_map/psum | solution.py:128
  8.2 10.2 %collective-permute-start = (f32[2,32,256]{2,1,0:T(8,128)S(1)}, f32[2,32,256]{2,1,0:T(8,128)S(1)}, u32[]{:S(2)}, u32[]{:S(2)}) collective-permute-start(f32[2,32,256]{2,1,0:T(8,128)S(1)} %get-tuple-element.258), channel_id=1, source_target_pairs={{0,16},{16,32},{32,48},{48,64},{64,80},{80,96},{96,112},{112,128},... | collective-permute-start | bytes 196616 | tf_op jit(solution)/shard_map/ppermute | solution.py:19
  13.3 7.7 %collective-permute-start.1 = (f32[2,32,256]{2,1,0:T(8,128)S(1)}, f32[2,32,256]{2,1,0:T(8,128)S(1)}, u32[]{:S(2)}, u32[]{:S(2)}) collective-permute-start(f32[2,32,256]{2,1,0:T(8,128)S(1)} %get-tuple-element.257), channel_id=1, source_target_pairs={{16,0},{32,16},{48,32},{64,48},{80,64},{96,80},{112,96},{128,112},... | collective-permute-start | bytes 196616 | tf_op jit(solution)/shard_map/ppermute | solution.py:22
  21.9 8.7 %collective-permute-start.2 = (f32[2,320,32]{2,1,0:T(8,128)}, f32[2,320,32]{2,1,0:T(8,128)}, u32[]{:S(2)}, u32[]{:S(2)}) collective-permute-start(f32[2,320,32]{2,1,0:T(8,128)} %get-tuple-element.255), channel_id=1, source_target_pairs={{0,1},{1,2},{2,3},{3,4},{4,5},{5,6},{6,7},{7,8},{8,9},{9,10},{10,1... | collective-permute-start | bytes 245768 | tf_op jit(solution)/shard_map/ppermute | solution.py:19
  23.8 8.5 %collective-permute-start.3 = (f32[2,320,32]{2,1,0:T(8,128)}, f32[2,320,32]{2,1,0:T(8,128)}, u32[]{:S(2)}, u32[]{:S(2)}) collective-permute-start(f32[2,320,32]{2,1,0:T(8,128)} %get-tuple-element.256), channel_id=1, source_target_pairs={{1,0},{2,1},{3,2},{4,3},{5,4},{6,5},{7,6},{8,7},{9,8},{10,9},{11,1... | collective-permute-start | bytes 245768 | tf_op jit(solution)/shard_map/ppermute | solution.py:22
  27.7 8.3 %copy-start = (f32[2,256,256]{2,1,0:T(8,128)S(1)}, f32[2,256,256]{2,1,0:T(8,128)}, u32[]{:S(2)}) copy-start(f32[2,256,256]{2,1,0:T(8,128)} %param.7) | copy-start | bytes 1572868
  27.7 8.3 %copy-start.6 = (s32[1,1,4,2]{2,3,1,0:T(2,128)S(1)}, s32[1,1,4,2]{2,3,1,0:T(2,128)}, u32[]{:S(2)}) copy-start(s32[1,1,4,2]{2,3,1,0:T(2,128)} %param.9) | copy-start | bytes 100
  48.9 1.2 copy-start.1
  76.0 1.2 copy-start.1
  103.1 1.2 copy-start.1
  130.2 1.2 copy-start.1
  144.5 8.4 %collective-permute-start.4 = (f32[3,32,320]{2,1,0:T(8,128)S(1)}, f32[3,32,320]{2,1,0:T(8,128)S(1)}, u32[]{:S(2)}, u32[]{:S(2)}) collective-permute-start(f32[3,32,320]{2,1,0:T(8,128)S(1)} %get-tuple-element.249), channel_id=1, source_target_pairs={{0,16},{16,32},{32,48},{48,64},{64,80},{80,96},{96,112},{112,128},... | collective-permute-start | bytes 368648 | tf_op jit(solution)/shard_map/ppermute | solution.py:30
  149.8 16.5 %copy-start.2 = (f32[4,256,256]{2,1,0:T(8,128)S(1)}, f32[4,256,256]{2,1,0:T(8,128)}, u32[]{:S(2)}) copy-start(f32[4,256,256]{2,1,0:T(8,128)} %get-tuple-element.408) | copy-start | bytes 3145732
  149.8 9.4 %collective-permute-start.5 = (f32[3,32,320]{2,1,0:T(8,128)S(1)}, f32[3,32,320]{2,1,0:T(8,128)S(1)}, u32[]{:S(2)}, u32[]{:S(2)}) collective-permute-start(f32[3,32,320]{2,1,0:T(8,128)S(1)} %get-tuple-element.250), channel_id=1, source_target_pairs={{16,0},{32,16},{48,32},{64,48},{80,64},{96,80},{112,96},{128,112},... | collective-permute-start | bytes 368648 | tf_op jit(solution)/shard_map/ppermute | solution.py:30
  160.8 88.7 %collective-permute-start.6 = (f32[3,256,32]{2,1,0:T(8,128)S(1)}, f32[3,256,32]{2,1,0:T(8,128)S(1)}, u32[]{:S(2)}, u32[]{:S(2)}) collective-permute-start(f32[3,256,32]{2,1,0:T(8,128)S(1)} %get-tuple-element.251), channel_id=1, source_target_pairs={{0,1},{1,2},{2,3},{3,4},{4,5},{5,6},{6,7},{7,8},{8,9},{9,10},{10,1... | collective-permute-start | bytes 294920 | tf_op jit(solution)/shard_map/ppermute | solution.py:30
  163.4 86.2 %collective-permute-start.7 = (f32[3,256,32]{2,1,0:T(8,128)S(1)}, f32[3,256,32]{2,1,0:T(8,128)S(1)}, u32[]{:S(2)}, u32[]{:S(2)}) collective-permute-start(f32[3,256,32]{2,1,0:T(8,128)S(1)} %get-tuple-element.252), channel_id=1, source_target_pairs={{1,0},{2,1},{3,2},{4,3},{5,4},{6,5},{7,6},{8,7},{9,8},{10,9},{11,1... | collective-permute-start | bytes 294920 | tf_op jit(solution)/shard_map/ppermute | solution.py:30
  249.5 1.0 copy-start.4
  505.2 3.6 copy-start.5
Sparse Core Ops, SparseCore 0:
  249.6 255.4 all-reduce.5
where the time goes:
time: 519 us; the launch traced here: 516 us
  waiting for transfers between devices  269 us (52%)
  blocking collectives  81.6 us (16%)
  local copies, waits for them, and re-layouts  45.4 us (9%)
  other arithmetic  41.4 us (8%)
  starting transfers between devices  24.3 us (5%)
  matrix products  23.4 us (5%)
  loops' own time  15.9 us (3%)
  between operations  15.6 us (3%)
    psum x1, waiting for transfers between devices, per_device(): totals, target_sum = lax.psum((probe_acc, local_target), ('row', 'col'))  254 us
    psum x1, blocking collectives, per_device(): totals, target_sum = lax.psum((probe_acc, local_target), ('row', 'col'))  81.6 us
    dynamic_update_slice x4, local copies, waits for them, and re-layouts, visit(): lax.dynamic_update_slice(canvas, current + update, (anchor, offset[0], of...  33.4 us
    another operation x1, loops' own time, per_device(): lax.fori_loop(0, frame_total, visit, (canvas_start, probe_start))  15.9 us
    dot_general x8, matrix products, transform(): mixed = jnp.dot(left_matrix, stacked, precision=lax.Precision.HIGHEST)  14.9 us
    add x4, other arithmetic, visit(): current + update  12.6 us
    ppermute x4, starting transfers between devices, shifted(): return lax.ppermute(block, axis, route)  12.3 us
  transfers between devices with their start and end apart: 9, of which 6 were waited for; matrix products, arithmetic and copies ran while one was open for 1% of the time, Pallas kernels for 0%

commit v1 on v0

--- a/solution.py
+++ b/solution.py
@@ -125,7 +125,7 @@
     local_target = jnp.sum(measured * measured)
     devices = lax.axis_size("row") * lax.axis_size("col")
     frame_count = frame_total * devices
-    totals, target_sum = lax.psum((probe_acc, local_target), ("row", "col"))
+    totals, target_sum = lax.psum(lax.psum((probe_acc, local_target), "row"), "col")
     stepped = probe + totals[0:2] / (totals[2] + regular)
     probe_power = jnp.sum(stepped * stepped)
     target = target_sum / frame_count

time: 519 us -> 453 us (0.87)
  waiting for transfers between devices: 269 us -> 213 us
  blocking collectives: 81.6 us -> 65.8 us
    psum x1 -> x2, waiting for transfers between devices: 254 us -> 198 us  [the longest x1 147 us: per_device(): lax.psum((probe_acc, local_target), 'row')]
    psum x1 -> x2, blocking collectives: 81.6 us -> 65.8 us  [the longest x1 41.8 us: per_device(): lax.psum((probe_acc, local_target), 'row')]
  transfers between devices with their start and end apart: 9 -> 10, of which waited for: 6 -> 7; matrix products, arithmetic and copies ran while one was open for 1% -> 2% of each run, Pallas kernels for 0% -> 0%
where the time goes in v1:
time: 453 us; the launch traced here: 447 us
  waiting for transfers between devices  213 us (47%)
  blocking collectives  65.8 us (15%)
  local copies, waits for them, and re-layouts  44.8 us (10%)
  other arithmetic  43.5 us (10%)
  starting transfers between devices  24.2 us (5%)
  matrix products  23.4 us (5%)
  loops' own time  15.9 us (4%)
  between operations  15.6 us (3%)
    psum x1, waiting for transfers between devices, per_device(): lax.psum((probe_acc, local_target), 'row')  147 us
    psum x1, waiting for transfers between devices, per_device(): lax.psum(lax.psum((probe_acc, local_target), 'row'), 'col')  51.4 us
    psum x1, blocking collectives, per_device(): lax.psum((probe_acc, local_target), 'row')  41.8 us
    dynamic_update_slice x4, local copies, waits for them, and re-layouts, visit(): lax.dynamic_update_slice(canvas, current + update, (anchor, offset[0], of...  33.4 us
    psum x1, blocking collectives, per_device(): lax.psum(lax.psum((probe_acc, local_target), 'row'), 'col')  23.9 us
    another operation x1, loops' own time, per_device(): lax.fori_loop(0, frame_total, visit, (canvas_start, probe_start))  15.9 us
    dot_general x8, matrix products, transform(): mixed = jnp.dot(left_matrix, stacked, precision=lax.Precision.HIGHEST)  14.9 us
    add x4, other arithmetic, visit(): current + update  12.5 us
  transfers between devices with their start and end apart: 10, of which 7 were waited for; matrix products, arithmetic and copies ran while one was open for 2% of the time, Pallas kernels for 0%

profile of v1, /device:TPU:2, one launch (start us, length us, event | category | flops | bytes accessed | tf_op | source)
XLA Modules:
  0.0 446.6 jit_solution(11396383427636254170)
XLA Ops:
  8.2 5.1 %collective-permute-start = (f32[2,32,256]{2,1,0:T(8,128)S(1)}, f32[2,32,256]{2,1,0:T(8,128)S(1)}, u32[]{:S(2)}, u32[]{:S(2)}) collective-permute-start(f32[2,32,256]{2,1,0:T(8,128)S(1)} %get-tuple-element.258), channel_id=1, source_target_pairs={{0,16},{16,32},{32,48},{48,64},{64,80},{80,96},{96,112},{112,128},... | collective-permute-start | bytes 196616 | tf_op jit(solution)/shard_map/ppermute | solution.py:19
  18.4 2.5 collective-permute-done.1
  21.9 1.9 collective-permute-start.2
  23.8 3.6 collective-permute-start.3
  27.7 2.9 collective-permute-done.2
  32.3 2.4 pad_maximum_fusion.5
  36.0 107.5 %while.16 = (s32[]{:T(128)}, f32[3,320,320]{2,1,0:T(8,128)}, f32[3,256,256]{2,1,0:T(8,128)}, s32[4,2]{0,1:T(2,128)S(1)}, f32[2,256,256]{2,1,0:T(8,128)S(1)}, /*i...) while((s32[]{:T(128)}, f32[3,320,320]{2,1,0:T(8,128)}, ...), condition=%wide.region_1.2_spmd.clone, body=%wide.region_0.1_spmd.clone.sunk | while | flops 3225354240 | bytes 31064388 | solution.py:113
  41.8 1.9 convolution_bitcast_fusion.4
  45.9 1.9 convolution_bitcast_fusion.5
  51.4 2.9 maximum_add_fusion.3
  54.3 8.8 %dynamic_update_slice.9 = f32[3,320,320]{2,1,0:T(8,128)} dynamic-update-slice(f32[3,320,320]{2,1,0:T(8,128)} %get-tuple-element.377, f32[3,256,256]{2,1,0:T(8,128)S(1)} %get-tuple-element.360, s32[]{:T(128)} %constant.57.clone.1..sunk, s32[]{:T(128)S(6)} %select_n.61, s32[]{:T(128)S(6)} %select_n.62) | dynamic-update-slice | bytes 1572868 | tf_op jit(solution)/shard_map/while/body/eval_jaxpr/dynamic_update_slice | solution.py:108
  68.9 1.9 convolution_bitcast_fusion.4
  73.0 1.9 convolution_bitcast_fusion.5
  78.4 3.2 maximum_add_fusion.3
  81.6 8.5 %dynamic_update_slice.9 = f32[3,320,320]{2,1,0:T(8,128)} dynamic-update-slice(f32[3,320,320]{2,1,0:T(8,128)} %get-tuple-element.377, f32[3,256,256]{2,1,0:T(8,128)S(1)} %get-tuple-element.360, s32[]{:T(128)} %constant.57.clone.1..sunk, s32[]{:T(128)S(6)} %select_n.61, s32[]{:T(128)S(6)} %select_n.62) | dynamic-update-slice | bytes 1572868 | tf_op jit(solution)/shard_map/while/body/eval_jaxpr/dynamic_update_slice | solution.py:108
  96.0 1.9 convolution_bitcast_fusion.4
  100.1 1.9 convolution_bitcast_fusion.5
  105.5 3.2 maximum_add_fusion.3
  108.7 8.5 %dynamic_update_slice.9 = f32[3,320,320]{2,1,0:T(8,128)} dynamic-update-slice(f32[3,320,320]{2,1,0:T(8,128)} %get-tuple-element.377, f32[3,256,256]{2,1,0:T(8,128)S(1)} %get-tuple-element.360, s32[]{:T(128)} %constant.57.clone.1..sunk, s32[]{:T(128)S(6)} %select_n.61, s32[]{:T(128)S(6)} %select_n.62) | dynamic-update-slice | bytes 1572868 | tf_op jit(solution)/shard_map/while/body/eval_jaxpr/dynamic_update_slice | solution.py:108
  123.1 1.9 convolution_bitcast_fusion.4
  127.2 1.9 convolution_bitcast_fusion.5
  132.7 3.2 maximum_add_fusion.3
  135.8 7.6 %dynamic_update_slice.9 = f32[3,320,320]{2,1,0:T(8,128)} dynamic-update-slice(f32[3,320,320]{2,1,0:T(8,128)} %get-tuple-element.377, f32[3,256,256]{2,1,0:T(8,128)S(1)} %get-tuple-element.360, s32[]{:T(128)} %constant.57.clone.1..sunk, s32[]{:T(128)S(6)} %select_n.61, s32[]{:T(128)S(6)} %select_n.62) | dynamic-update-slice | bytes 1572868 | tf_op jit(solution)/shard_map/while/body/eval_jaxpr/dynamic_update_slice | solution.py:108
  144.5 5.3 %collective-permute-start.4 = (f32[3,32,320]{2,1,0:T(8,128)S(1)}, f32[3,32,320]{2,1,0:T(8,128)S(1)}, u32[]{:S(2)}, u32[]{:S(2)}) collective-permute-start(f32[3,32,320]{2,1,0:T(8,128)S(1)} %get-tuple-element.249), channel_id=1, source_target_pairs={{0,16},{16,32},{32,48},{48,64},{64,80},{80,96},{96,112},{112,128},... | collective-permute-start | bytes 368648 | tf_op jit(solution)/shard_map/ppermute | solution.py:30
  153.0 6.2 %collective-permute-done.5 = f32[3,32,320]{2,1,0:T(8,128)S(1)} collective-permute-done((f32[3,32,320]{2,1,0:T(8,128)S(1)}, f32[3,32,320]{2,1,0:T(8,128)S(1)}, u32[]{:S(2)}, u32[]{:S(2)}) %collective-permute-start.5) | collective-permute-done | bytes 122912 | tf_op jit(solution)/shard_map/ppermute | solution.py:30
  160.7 2.5 collective-permute-start.6
  163.3 3.0 collective-permute-start.7
  166.3 146.6 %all-reduce.7.cloned.1.call-done = f32[3,256,256]{2,1,0:T(8,128)} async-done(((f32[3,256,256]{2,1,0:T(8,128)}), f32[3,256,256]{2,1,0:T(8,128)}) %all-reduce.7.cloned.1.call-update) | async-done | bytes 786448 | tf_op jit(solution)/shard_map/psum | solution.py:128
  313.0 2.1 multiply_reduce_fusion
  315.1 41.8 %psum.30 = f32[]{:T(128)} all-reduce(f32[]{:T(128)} %multiply_reduce_fusion), channel_id=1, replica_groups=mesh['row'=16,'col'=16] {'row'}, use_global_device_ids=true, to_apply=%region_5.6 | all-reduce | flops 1 | bytes 8 | tf_op jit(solution)/shard_map/psum | solution.py:128
  356.9 23.9 %psum.31 = f32[]{:T(128)} all-reduce(f32[]{:T(128)} %psum.30), channel_id=1, replica_groups=mesh['row'=16,'col'=16] {'col'}, use_global_device_ids=true, to_apply=%region_6.7 | all-reduce | flops 1 | bytes 8 | tf_op jit(solution)/shard_map/psum | solution.py:128
  383.8 51.4 %all-reduce.9.cloned.1.call-done = f32[3,256,256]{2,1,0:T(8,128)} async-done(((f32[3,256,256]{2,1,0:T(8,128)}), f32[3,256,256]{2,1,0:T(8,128)}) %all-reduce.9.cloned.1.call-update) | async-done | bytes 786448 | tf_op jit(solution)/shard_map/psum | solution.py:128
  (101 shorter events, 52.7 us)
Async XLA Ops:
  7.2 11.2 %copy-start.2 = (f32[2,256,256]{2,1,0:T(8,128)S(1)}, f32[2,256,256]{2,1,0:T(8,128)}, u32[]{:S(2)}) copy-start(f32[2,256,256]{2,1,0:T(8,128)} %param.6) | copy-start | bytes 1572868
  7.2 305.8 %all-reduce.7.cloned.1.call-start = ((), (), s32[]{:S(2)}) async-start(), calls=%async_computation | async-start | bytes 1572864 | tf_op jit(solution)/shard_map/psum | solution.py:128
  8.2 10.2 %collective-permute-start = (f32[2,32,256]{2,1,0:T(8,128)S(1)}, f32[2,32,256]{2,1,0:T(8,128)S(1)}, u32[]{:S(2)}, u32[]{:S(2)}) collective-permute-start(f32[2,32,256]{2,1,0:T(8,128)S(1)} %get-tuple-element.258), channel_id=1, source_target_pairs={{0,16},{16,32},{32,48},{48,64},{64,80},{80,96},{96,112},{112,128},... | collective-permute-start | bytes 196616 | tf_op jit(solution)/shard_map/ppermute | solution.py:19
  13.3 7.7 %collective-permute-start.1 = (f32[2,32,256]{2,1,0:T(8,128)S(1)}, f32[2,32,256]{2,1,0:T(8,128)S(1)}, u32[]{:S(2)}, u32[]{:S(2)}) collective-permute-start(f32[2,32,256]{2,1,0:T(8,128)S(1)} %get-tuple-element.257), channel_id=1, source_target_pairs={{16,0},{32,16},{48,32},{64,48},{80,64},{96,80},{112,96},{128,112},... | collective-permute-start | bytes 196616 | tf_op jit(solution)/shard_map/ppermute | solution.py:22
  21.9 8.7 %collective-permute-start.2 = (f32[2,320,32]{2,1,0:T(8,128)}, f32[2,320,32]{2,1,0:T(8,128)}, u32[]{:S(2)}, u32[]{:S(2)}) collective-permute-start(f32[2,320,32]{2,1,0:T(8,128)} %get-tuple-element.255), channel_id=1, source_target_pairs={{0,1},{1,2},{2,3},{3,4},{4,5},{5,6},{6,7},{7,8},{8,9},{9,10},{10,1... | collective-permute-start | bytes 245768 | tf_op jit(solution)/shard_map/ppermute | solution.py:19
  23.8 8.5 %collective-permute-start.3 = (f32[2,320,32]{2,1,0:T(8,128)}, f32[2,320,32]{2,1,0:T(8,128)}, u32[]{:S(2)}, u32[]{:S(2)}) collective-permute-start(f32[2,320,32]{2,1,0:T(8,128)} %get-tuple-element.256), channel_id=1, source_target_pairs={{1,0},{2,1},{3,2},{4,3},{5,4},{6,5},{7,6},{8,7},{9,8},{10,9},{11,1... | collective-permute-start | bytes 245768 | tf_op jit(solution)/shard_map/ppermute | solution.py:22
  27.7 8.3 %copy-start = (f32[2,256,256]{2,1,0:T(8,128)S(1)}, f32[2,256,256]{2,1,0:T(8,128)}, u32[]{:S(2)}) copy-start(f32[2,256,256]{2,1,0:T(8,128)} %param.7) | copy-start | bytes 1572868
  27.7 8.3 %copy-start.5 = (s32[1,1,4,2]{2,3,1,0:T(2,128)S(1)}, s32[1,1,4,2]{2,3,1,0:T(2,128)}, u32[]{:S(2)}) copy-start(s32[1,1,4,2]{2,3,1,0:T(2,128)} %param.9) | copy-start | bytes 100
  48.9 1.2 copy-start.1
  76.0 1.2 copy-start.1
  103.1 1.2 copy-start.1
  130.2 1.2 copy-start.1
  143.5 291.8 %all-reduce.9.cloned.1.call-start = ((), (), s32[]{:S(2)}) async-start(), calls=%async_computation.1 | async-start | bytes 1572864 | tf_op jit(solution)/shard_map/psum | solution.py:128
  144.5 8.5 %collective-permute-start.4 = (f32[3,32,320]{2,1,0:T(8,128)S(1)}, f32[3,32,320]{2,1,0:T(8,128)S(1)}, u32[]{:S(2)}, u32[]{:S(2)}) collective-permute-start(f32[3,32,320]{2,1,0:T(8,128)S(1)} %get-tuple-element.249), channel_id=1, source_target_pairs={{0,16},{16,32},{32,48},{48,64},{64,80},{80,96},{96,112},{112,128},... | collective-permute-start | bytes 368648 | tf_op jit(solution)/shard_map/ppermute | solution.py:30
  149.9 9.3 %collective-permute-start.5 = (f32[3,32,320]{2,1,0:T(8,128)S(1)}, f32[3,32,320]{2,1,0:T(8,128)S(1)}, u32[]{:S(2)}, u32[]{:S(2)}) collective-permute-start(f32[3,32,320]{2,1,0:T(8,128)S(1)} %get-tuple-element.250), channel_id=1, source_target_pairs={{16,0},{32,16},{48,32},{64,48},{80,64},{96,80},{112,96},{128,112},... | collective-permute-start | bytes 368648 | tf_op jit(solution)/shard_map/ppermute | solution.py:30
  160.7 220.8 %collective-permute-start.6 = (f32[3,256,32]{2,1,0:T(8,128)S(1)}, f32[3,256,32]{2,1,0:T(8,128)S(1)}, u32[]{:S(2)}, u32[]{:S(2)}) collective-permute-start(f32[3,256,32]{2,1,0:T(8,128)S(1)} %get-tuple-element.251), channel_id=1, source_target_pairs={{0,1},{1,2},{2,3},{3,4},{4,5},{5,6},{6,7},{7,8},{8,9},{9,10},{10,1... | collective-permute-start | bytes 294920 | tf_op jit(solution)/shard_map/ppermute | solution.py:30
  163.3 218.3 %collective-permute-start.7 = (f32[3,256,32]{2,1,0:T(8,128)S(1)}, f32[3,256,32]{2,1,0:T(8,128)}, u32[]{:S(2)}, u32[]{:S(2)}) collective-permute-start(f32[3,256,32]{2,1,0:T(8,128)S(1)} %get-tuple-element.252), channel_id=1, source_target_pairs={{1,0},{2,1},{3,2},{4,3},{5,4},{6,5},{7,6},{8,7},{9,8},{10,9},{11,1... | collective-permute-start | bytes 294920 | tf_op jit(solution)/shard_map/ppermute | solution.py:30
  315.1 67.9 %copy-start.3 = (f32[2,256,256]{2,1,0:T(8,128)S(1)}, f32[2,256,256]{2,1,0:T(8,128)}, u32[]{:S(2)}) copy-start(f32[2,256,256]{2,1,0:T(8,128)} %param.6) | copy-start | bytes 1572868
  435.3 3.6 copy-start.4
Sparse Core Ops, SparseCore 0:
  143.6 169.3 all-reduce.6
  315.5 119.6 all-reduce.8
